TPU v7x, 32 devices: a whole 2x2x4 slice. The times are simulated.
32 devices in a mesh: rays: 8 (over z, x), views: 4 (over y, core).
Axes of the slice: x: 2, y: 2, z: 4, core: 2. Of those that a mesh axis runs over, the one named last changes fastest.
Arguments:
- master: float32 [11384], P('rays')
- first_moment: float32 [11384], P('rays'), may hold values from -0.75 to 0.75
- second_moment: float32 [11384], P('rays'), may hold values from 0.001 to 0.01
- step_count: int32 [1], replicated, may hold values from 2 to 20
- feature_maps: bfloat16 [12, 35, 12032], P('views'), may hold values from -6 to 6
- pixel_index: int32 [24576, 12], P('rays', 'views'), may hold values from 0 to 12031
- visible: int32 [24576, 12], P('rays', 'views'), may hold values from 0 to 1, as said below
- deltas: float32 [128, 192], P('rays'), may hold values from 0.002 to 0.02
- targets: float32 [128, 3], P('rays'), may hold values from -3 to 3
- scene_id: int32 [128], P('rays'), may hold values from 0 to 7
- scene_weight: int32 [8], replicated, may hold values from 1 to 4
Outputs:
- loss: float32 [], replicated
- master_new: float32 [11384], P('rays')
- first_new: float32 [11384], P('rays')
- second_new: float32 [11384], P('rays')
Inputs may be any that keep to these rules, and one draw needn't show every extreme that they name: Every sample is visible in at least one of the first 10 view slots; the last two slots are never visible.
All inputs are finite; a program needn't handle non-finite values.
Results may differ from a plain program's by a relative error of at most 0.00077.
Values may be sent and summed in bfloat16 or wider, within the bound.
No kernel may reach another device: no remote copies, remote signals or barrier semaphores. Data moves between devices by JAX's collectives and lax.ppermute only.
A program may use at most 128 MiB of HBM per device.

v0:
```python
import math
import jax
import jax.numpy as jnp
from jax import lax
from jax.sharding import PartitionSpec as P

MICRO = 2
LAYOUT = (
    ("w1", (35, 64)),
    ("b1", (64,)),
    ("w2", (64, 32)),
    ("b2", (32,)),
    ("u1", (64, 32)),
    ("c1", (32,)),
    ("u2", (32, 16)),
    ("c2", (16,)),
    ("wq", (16, 64)),
    ("wk", (16, 64)),
    ("wv", (16, 64)),
    ("wo", (64, 16)),
    ("s1", (16, 16)),
    ("d1", (16,)),
    ("s2", (16, 1)),
    ("d2", (1,)),
)
MOMENT_DECAY = 0.5
SQUARE_DECAY = 0.5
LEARNING_RATE = 0.05
WEIGHT_DECAY = 0.01
EPSILON = 1e-08


def rounded(value, ledger):
    if "give" in ledger:
        return value + ledger["give"].pop(0)
    narrow = lax.optimization_barrier(value.astype(jnp.bfloat16)).astype(jnp.float32)
    ledger["keep"].append(narrow - value)
    return narrow


def matmul_low(left_op, right_op):
    return jnp.matmul(left_op, right_op, precision=lax.Precision.HIGHEST)


def traced(part_fn, *primals):
    record = {"keep": []}
    part_fn(record, *primals)
    offsets = record["keep"]
    return jax.vjp(lambda *values: part_fn({"give": list(offsets)}, *values), *primals)


def unpack(flat_params):
    params = {}
    offset = 0
    for section, section_dims in LAYOUT:
        amount = math.prod(section_dims)
        params[section] = flat_params[offset : offset + amount].reshape(section_dims)
        offset = offset + amount
    return params


def views_part(ledger, params, features_in, visible_f):
    hidden = rounded(jax.nn.elu(matmul_low(features_in, params["w1"]) + params["b1"]), ledger)
    feature = jax.nn.elu(matmul_low(hidden, params["w2"]) + params["b2"])
    weighted = visible_f[..., None] * feature
    return (feature, jnp.sum(weighted, axis=1), jnp.sum(weighted * feature, axis=1))


def moments(total_sum, total_square, seen_count):
    average = total_sum / seen_count[:, None]
    return (average, total_square / seen_count[:, None] - average * average)


def blend_part(ledger, params, feature, average, variance, colour_in, visible_f):
    spread_cols = jnp.broadcast_to(variance[:, None, :], feature.shape)
    joined = rounded(jnp.concatenate([feature - average[:, None, :], spread_cols], axis=-1), ledger)
    inner_act = rounded(jax.nn.elu(matmul_low(joined, params["u1"]) + params["c1"]), ledger)
    logits = matmul_low(inner_act, params["u2"]) + params["c2"]
    exponent = visible_f[..., None] * jnp.exp(logits)
    numerator = jnp.sum(exponent * feature[..., :16], axis=1)
    denominator = jnp.sum(exponent, axis=1)
    colour_sum = jnp.sum(exponent[..., :1] * colour_in, axis=1)
    return (numerator, denominator, colour_sum)


def ray_part(ledger, params, numerator, denominator, colour_sum, deltas, targets, ray_weight):
    ray_count, samples = deltas.shape
    tokens = numerator / denominator
    colour = (colour_sum / denominator[:, :1]).reshape(ray_count, samples, 3)
    token_low = rounded(tokens, ledger)
    queries = rounded(matmul_low(token_low, params["wq"]), ledger).reshape(
        ray_count, samples, 4, 16
    )
    key_rows = rounded(matmul_low(token_low, params["wk"]), ledger).reshape(
        ray_count, samples, 4, 16
    )
    val_rows = rounded(matmul_low(token_low, params["wv"]), ledger).reshape(
        ray_count, samples, 4, 16
    )
    scores = (
        jnp.einsum("rqhd,rkhd->rhqk", queries, key_rows, precision=lax.Precision.HIGHEST) * 0.25
    )
    attention = rounded(jax.nn.softmax(scores, axis=-1), ledger)
    attended = jnp.einsum("rhqk,rkhd->rqhd", attention, val_rows, precision=lax.Precision.HIGHEST)
    attended = rounded(attended.reshape(ray_count * samples, 64), ledger)
    mixed_rows = tokens + matmul_low(attended, params["wo"])
    mixed_low = rounded(mixed_rows, ledger)
    inner_act = rounded(jax.nn.elu(matmul_low(mixed_low, params["s1"]) + params["d1"]), ledger)
    density = jax.nn.softplus(matmul_low(inner_act, params["s2"])[:, 0] + params["d2"][0])
    optical = density.reshape(ray_count, samples) * deltas
    before = jnp.cumsum(optical, axis=1) - optical
    render_weight = jnp.exp(-before) * (1.0 - jnp.exp(-optical))
    pixel_colour = jnp.sum(render_weight[..., None] * colour, axis=1)
    return jnp.sum(ray_weight * jnp.sum((pixel_colour - targets) ** 2, axis=-1))


def adamw(master, first_moment, second_moment, gradient, step_count):
    step_float = step_count[0].astype(jnp.float32)
    first_new = MOMENT_DECAY * first_moment + (1.0 - MOMENT_DECAY) * gradient
    second_new = SQUARE_DECAY * second_moment + (1.0 - SQUARE_DECAY) * gradient * gradient
    first_fix = 1.0 - jnp.power(MOMENT_DECAY, step_float)
    second_fix = 1.0 - jnp.power(SQUARE_DECAY, step_float)
    update = first_new / first_fix / (jnp.sqrt(second_new / second_fix) + EPSILON)
    master_new = master - LEARNING_RATE * (update + WEIGHT_DECAY * master)
    return (master_new, first_new, second_new)


def fetch(master):
    narrow = master.astype(jnp.bfloat16)
    return lax.all_gather(narrow, "rays", axis=0, tiled=True).astype(jnp.float32)


def body(
    master,
    first_moment,
    second_moment,
    step_count,
    feature_maps,
    pixel_index,
    visible,
    deltas,
    targets,
    scene_id,
    scene_weight,
):
    view_devices = lax.axis_size("views")
    ray_rows, samples = deltas.shape
    per_batch = ray_rows // MICRO
    point_rows = per_batch * samples
    visible_f = visible.astype(jnp.float32)
    view_slot = jnp.arange(feature_maps.shape[0])[None, :]
    scene_hits = (scene_id[:, None] == jnp.arange(scene_weight.shape[0])[None, :]).astype(
        jnp.float32
    )
    ray_weight = jnp.sum(scene_hits * scene_weight.astype(jnp.float32)[None, :], axis=1)
    weight_part = jnp.sum(ray_weight)
    seed = 1.0 / lax.psum(weight_part, "rays")
    gradient = jnp.zeros((master.shape[0] * lax.axis_size("rays"),), jnp.float32)
    loss_part = jnp.zeros((), jnp.float32)
    for batch_index in range(MICRO):
        flat_w = fetch(master)
        start = batch_index * point_rows
        ray_start = batch_index * per_batch
        vis_rows = visible_f[start : start + point_rows]
        features_in = feature_maps[view_slot, :, pixel_index[start : start + point_rows]].astype(
            jnp.float32
        )
        colour_in = features_in[..., 32:]
        seen_part = jnp.sum(vis_rows, axis=1)
        delta_rows = deltas[ray_start : ray_start + per_batch]
        target_rows = targets[ray_start : ray_start + per_batch]
        weight_rows = ray_weight[ray_start : ray_start + per_batch]
        (feature, total_sum, total_square), back_views = traced(
            lambda ledger, flat_params: views_part(
                ledger, unpack(flat_params), features_in, vis_rows
            ),
            flat_w,
        )
        whole_sum, whole_square, whole_seen = lax.psum(
            (total_sum, total_square, seen_part), "views"
        )
        (average, variance), back_moments = jax.vjp(
            lambda sum_val, square_val: moments(sum_val, square_val, whole_seen),
            whole_sum,
            whole_square,
        )
        (numerator, denominator, colour_sum), back_blend = traced(
            lambda ledger, flat_params, feature_val, average_val, variance_val: blend_part(
                ledger,
                unpack(flat_params),
                feature_val,
                average_val,
                variance_val,
                colour_in,
                vis_rows,
            ),
            flat_w,
            feature,
            average,
            variance,
        )
        numerator, denominator, colour_sum = lax.psum((numerator, denominator, colour_sum), "views")
        batch_loss, back_rays = traced(
            lambda ledger, flat_params, numer_val, denom_val, colour_val: ray_part(
                ledger,
                unpack(flat_params),
                numer_val,
                denom_val,
                colour_val,
                delta_rows,
                target_rows,
                weight_rows,
            ),
            flat_w,
            numerator,
            denominator,
            colour_sum,
        )
        loss_part = loss_part + batch_loss
        grad_ray_w, grad_numer, grad_denom, grad_colour = back_rays(seed)
        grad_blend_w, grad_feature, grad_average, grad_variance = back_blend(
            (grad_numer, grad_denom, grad_colour)
        )
        own_gsum, own_gsquare = back_moments((grad_average, grad_variance))
        grad_sum, grad_square = (
            lax.psum(own_gsum.astype(jnp.bfloat16), "views").astype(jnp.float32),
            lax.psum(own_gsquare.astype(jnp.bfloat16), "views").astype(jnp.float32),
        )
        (grad_view_w,) = back_views((grad_feature, grad_sum, grad_square))
        gradient = gradient + grad_view_w + grad_blend_w + grad_ray_w / view_devices
    owned_grad = lax.psum_scatter(gradient, "rays", scatter_dimension=0, tiled=True)
    owned_grad = lax.psum(owned_grad, "views")
    loss = lax.psum(loss_part, "rays") * seed
    master_new, first_new, second_new = adamw(
        master, first_moment, second_moment, owned_grad, step_count
    )
    return (loss, master_new, first_new, second_new)


def solution(mesh):
    placed = (
        P("rays"),
        P("rays"),
        P("rays"),
        P(),
        P("views", None, None),
        P("rays", "views"),
        P("rays", "views"),
        P("rays", None),
        P("rays", None),
        P("rays"),
        P(),
    )
    return jax.shard_map(
        body,
        mesh=mesh,
        in_specs=placed,
        out_specs=(P(), P("rays"), P("rays"), P("rays")),
        check_vma=False,
    )
```

profile of v0, /device:TPU:0, one launch (start us, length us, event | category | flops | bytes accessed | tf_op | source)
XLA Modules:
  0.0 687.4 jit_solution(12218807392890689628)
XLA Ops:
  10.2 38.8 %all-reduce.42 = bf16[11384]{0:T(1024)(128)(2,1)S(1)} all-reduce(bf16[11384]{0:T(1024)(128)(2,1)S(1)} %dynamic-update-slice), channel_id=1, replica_groups=mesh['rays'=8,'views'=4] {'rays'}, use_global_device_ids=true, to_apply=%add.42 | all-reduce | flops 11384 | bytes 45536
  50.5 8.5 %copy.206 = bf16[3,35,12032]{1,2,0:T(8,128)(2,1)} copy(bf16[3,35,12032]{2,1,0:T(8,128)(2,1)} %param.16) | data formatting | bytes 5053440 | tf_op args[4]
  59.8 54.4 %gather_fusion = bf16[4608,35]{1,0:T(8,128)(2,1)S(1)} fusion(bf16[3,35,12032]{1,2,0:T(8,128)(2,1)} %copy.206, s32[4608]{0:T(1024)S(1)} %reshape.470), kind=kCustom, calls=%fused_computation | custom fusion | bytes 681984 | tf_op jit(solution)/shard_map/gather | solution.py:165
  121.5 75.1 %gather_fusion.1 = bf16[4608,35]{1,0:T(8,128)(2,1)} fusion(bf16[3,35,12032]{1,2,0:T(8,128)(2,1)} %copy.206, s32[4608]{0:T(1024)S(1)} %reshape.476), kind=kCustom, calls=%fused_computation.1 | custom fusion | bytes 681984 | tf_op jit(solution)/shard_map/gather | solution.py:165
  196.7 3.3 reshape.479
  220.2 17.7 %psum.146 = f32[]{:T(128)} all-reduce(f32[]{:T(128)} %get-tuple-element.34), channel_id=1, replica_groups=mesh['rays'=8,'views'=4] {'rays'}, use_global_device_ids=true, to_apply=%region_45.47 | all-reduce | flops 1 | bytes 8 | tf_op jit(solution)/shard_map/psum | solution.py:157
  240.7 11.5 %all-reduce.46 = (f32[1536]{0:T(1024)}, f32[1536]{0:T(1024)}) all-reduce(f32[1536]{0:T(1024)} %get-tuple-element.28, f32[1536]{0:T(1024)} %get-tuple-element.29), channel_id=1, replica_groups=mesh['rays'=8,'views'=4] {'views'}, use_global_device_ids=true, to_apply=%region_25.27 | all-reduce | flops 3072 | bytes 24576 | tf_op jit(solution)/shard_map/psum | solution.py:179
  262.5 2.2 fusion.134
  271.7 10.6 %fusion.16 = f32[1536,3]{1,0:T(8,128)} fusion(f32[1536,3]{1,0:T(8,128)} %bitcast.363, bf16[1536,3,35]{2,1,0:T(4,128)(2,1)S(1)} %reshape.473), kind=kLoop, calls=%fused_computation.28 | loop fusion | flops 36864 | bytes 64512 | tf_op jit(solution)/shard_map/jvp()/reduce_sum | solution.py:82
  286.7 9.3 %fusion.18 = f32[1536,3]{1,0:T(8,128)} fusion(f32[1536,3]{1,0:T(8,128)S(1)} %bitcast.360, bf16[1536,3,35]{2,1,0:T(4,128)(2,1)S(1)} %reshape.479), kind=kLoop, calls=%fused_computation.30 | loop fusion | flops 36864 | bytes 64512 | tf_op jit(solution)/shard_map/jvp()/reduce_sum | solution.py:82
  296.1 36.2 %all-reduce.45 = (f32[1536,3]{1,0:T(8,128)}, f32[1536,3]{1,0:T(8,128)}) all-reduce(f32[1536,3]{1,0:T(8,128)} %fusion.18, f32[1536,3]{1,0:T(8,128)S(1)} %copy-done.63), channel_id=1, replica_groups=mesh['rays'=8,'views'=4] {'views'}, use_global_device_ids=true, to_apply=%region_39.41 | all-reduce | flops 9216 | bytes 73728 | tf_op jit(solution)/shard_map/psum | solution.py:202
  344.9 5.3 fusion.96
  350.2 5.3 fusion.258
  356.5 5.3 fusion.255
  362.7 2.0 subtract_add_fusion
  364.7 3.3 convolution_bitcast_fusion.9
  369.1 2.0 reshape.431
  381.3 5.5 fusion.104
  386.8 5.3 fusion.251
  393.2 5.3 fusion.248
  401.7 3.3 convolution_bitcast_fusion.11
  406.1 2.0 reshape.417
  421.5 2.3 multiply_reduce_fusion.8
  423.9 2.9 reduce-window.36
  427.0 2.3 multiply_reduce_fusion.9
  429.4 2.5 reduce-window.34
  435.0 9.0 %multiply_reduce_fusion.1 = (f32[8,4,192]{2,1,0:T(4,128)S(1)}, f32[8,4,192,192]{2,3,1,0:T(8,128)S(1)}) fusion(f32[8,4,192,192]{2,3,1,0:T(8,128)} %copy-done.3, f32[8,4,192]{2,1,0:T(4,128)S(1)} %copy-done.160, f32[8,4,16,192]{3,2,1,0:T(8,128)S(1)} %convolution_bitcast_fusion.7, f32[8,192,4,16]{1,0,3,2:T(8,128)S(1)} %copy-done.43), kind=kOutput, calls=%fused_computation.9 | convolution fusion | flops 230025216 | bytes 10272768 | tf_op jit(solution)/shard_map/transpose(jvp(rhqk,rkhd->rqhd))/dot_general | solution.py:104
  444.1 5.1 convolution_bitcast_fusion.4
  449.2 7.2 %convolution_bitcast_fusion.5 = f32[8,192,4,16]{1,3,2,0:T(8,128)} fusion(f32[8,192,4,16]{1,0,3,2:T(8,128)S(1)} %copy-done.78, f32[8,4,192,192]{2,3,1,0:T(8,128)S(1)} %bitcast.357, f32[8,4,192,192]{2,3,1,0:T(8,128)S(1)} %get-tuple-element.179, f32[8,4,192]{2,1,0:T(4,128)S(1)} %neg.100, f32[8,4,192]{2,1,0:T(4,128)S(1)} %copy-done.141), kind=kOutput, calls=%fused_computation.83 | convolution fusion | flops 231211008 | bytes 10272768 | tf_op jit(solution)/shard_map/transpose(jvp(rqhd,rkhd->rhqk))/dot_general | solution.py:101
  456.4 6.4 convolution_bitcast_fusion.6
  464.2 1.9 fusion.236
  469.5 8.9 %convolution_bitcast_fusion.2 = f32[8,192,4,16]{1,3,2,0:T(8,128)} fusion(f32[8,4,16,192]{3,2,1,0:T(8,128)S(1)} %convolution_bitcast_fusion.3, f32[8,4,192,192]{2,3,1,0:T(8,128)} %copy-done), kind=kOutput, calls=%fused_computation.80 | convolution fusion | flops 226492416 | bytes 5505024 | tf_op jit(solution)/shard_map/transpose(jvp(rhqk,rkhd->rqhd))/dot_general | solution.py:104
  478.5 6.2 multiply_reduce_fusion
  484.8 7.3 %convolution_bitcast_fusion.1 = f32[8,192,4,16]{1,3,2,0:T(8,128)} fusion(f32[8,192,4,16]{1,0,3,2:T(8,128)S(1)} %copy-done.74, f32[8,4,192,192]{2,3,1,0:T(8,128)S(1)} %bitcast.355, f32[8,4,192,192]{2,3,1,0:T(8,128)S(1)} %get-tuple-element.174, f32[8,4,192]{2,1,0:T(4,128)S(1)} %neg.109, f32[8,4,192]{2,1,0:T(4,128)S(1)} %copy-done.139), kind=kOutput, calls=%fused_computation.79 | convolution fusion | flops 231211008 | bytes 10272768 | tf_op jit(solution)/shard_map/transpose(jvp(rqhd,rkhd->rhqk))/dot_general | solution.py:101
  492.0 5.1 convolution_bitcast_fusion
  499.7 2.1 copy.249
  501.8 2.0 reshape.442
  507.1 5.5 fusion.17
  516.6 2.8 fusion.230
  529.9 3.8 fusion.19
  538.5 2.3 copy.271
  540.8 2.0 reshape.459
  546.0 2.5 fusion.235
  548.6 2.3 fusion.260
  590.3 29.1 %all-reduce.58.cloned.1.call-done = (bf16[1536,32]{0,1:T(8,128)(2,1)}, bf16[1536,32]{0,1:T(8,128)(2,1)}, bf16[1536,32]{0,1:T(8,128)(2,1)}, bf16[1536,32]{0,1:T(8,128)(2,1)}) async-done(((bf16[1536,32]{0,1:T(8,128)(2,1)}, bf16[1536,32]{0,1:T(8,128)(2,1)}, bf16[1536,32]{0,1:T(8,128)(2,1)}, bf16[1536,32]{0,1:T(8,128)(2,1)}), (bf16[1536,32]{0,1:T(8,128)(2,1)}, bf16[1536,32]{0,1:T(8,128)(2,1)}, ...) | async-done | bytes 393232 | tf_op jit(solution)/shard_map/psum | solution.py:226
  621.9 3.7 convolution_bitcast_fusion.15
  634.4 37.6 %all-reduce.44 = (f32[]{:T(128)}, f32[11384]{0:T(1024)S(1)}) all-reduce(f32[]{:T(128)S(6)} %add.408, f32[11384]{0:T(1024)S(1)} %multiply_add_fusion), channel_id=1, replica_groups=mesh['rays'=8,'views'=4] {'rays'}, use_global_device_ids=true, to_apply=%region_43.45 | all-reduce | flops 11385 | bytes 91080 | tf_op jit(solution)/shard_map/psum | solution.py:233
  672.1 5.9 psum.151
  (728 shorter events, 183.5 us)
Async XLA Ops:
  7.2 248.3 %all-reduce.56.cloned.1.call-start = ((), (), s32[]{:S(2)}) async-start(), calls=%async_computation.1 | async-start | bytes 1572864 | tf_op jit(solution)/shard_map/psum | solution.py:179
  115.0 156.7 %copy-start.6 = (bf16[1536,3,35]{2,1,0:T(4,128)(2,1)}, bf16[1536,3,35]{2,1,0:T(4,128)(2,1)S(1)}, u32[]{:S(2)}) copy-start(bf16[1536,3,35]{2,1,0:T(4,128)(2,1)S(1)} %reshape.473) | copy-start | bytes 967684
  120.8 85.9 %copy-start.110 = (f32[1536,3]{0,1:T(4,128)}, f32[1536,3]{0,1:T(4,128)S(1)}, u32[]{:S(2)}) copy-start(f32[1536,3]{0,1:T(4,128)S(1)} %get-tuple-element.97) | copy-start | bytes 55300
  200.0 86.7 %copy-start.4 = (bf16[1536,3,35]{2,1,0:T(4,128)(2,1)}, bf16[1536,3,35]{2,1,0:T(4,128)(2,1)S(1)}, u32[]{:S(2)}) copy-start(bf16[1536,3,35]{2,1,0:T(4,128)(2,1)S(1)} %reshape.479) | copy-start | bytes 967684
  207.8 124.5 %all-reduce.54.cloned.1.call-start = ((), (), s32[]{:S(2)}) async-start(), calls=%async_computation | async-start | bytes 786432 | tf_op jit(solution)/shard_map/psum | solution.py:202
  220.2 35.3 %copy-start.199 = (f32[16]{0:T(128)}, f32[16]{0:T(128)S(1)}, u32[]{:S(2)}) copy-start(f32[16]{0:T(128)S(1)} %get-tuple-element.35) | copy-start | bytes 196
  268.5 15.3 %copy-start.111 = (f32[1536,3]{0,1:T(4,128)S(1)}, f32[1536,3]{0,1:T(4,128)}, u32[]{:S(2)}) copy-start(f32[1536,3]{0,1:T(4,128)} %copy-done.110) | copy-start | bytes 55300
  271.7 10.6 %copy-start.25 = (f32[1536,3,32]{0,2,1:T(8,128)S(1)}, f32[1536,3,32]{0,2,1:T(8,128)}, u32[]{:S(2)}) copy-start(f32[1536,3,32]{0,2,1:T(8,128)} %copy-done.24) | copy-start | bytes 1769476
  271.7 10.6 %copy-start.70 = (f32[1536,3,32]{0,2,1:T(8,128)S(1)}, f32[1536,3,32]{0,2,1:T(8,128)}, u32[]{:S(2)}) copy-start(f32[1536,3,32]{0,2,1:T(8,128)} %get-tuple-element.138) | copy-start | bytes 1769476
  271.7 10.6 %copy-start.154 = (u8[1536,32]{0,1:T(8,128)(4,1)S(1)}, u8[1536,32]{0,1:T(8,128)(4,1)}, u32[]{:S(2)}) copy-start(u8[1536,32]{0,1:T(8,128)(4,1)} %get-tuple-element.137) | copy-start | bytes 147460
  271.7 12.0 %copy-start.68 = (f32[1536,3,32]{0,2,1:T(8,128)S(1)}, f32[1536,3,32]{0,2,1:T(8,128)}, u32[]{:S(2)}) copy-start(f32[1536,3,32]{0,2,1:T(8,128)} %get-tuple-element.82) | copy-start | bytes 1769476
  282.9 13.1 %copy-start.63 = (f32[1536,3]{1,0:T(8,128)S(1)}, f32[1536,3]{1,0:T(8,128)}, u32[]{:S(2)}) copy-start(f32[1536,3]{1,0:T(8,128)} %fusion.16) | copy-start | bytes 55300
  286.3 46.9 %copy-start.148 = (bf16[16,64]{1,0:T(8,128)(2,1)S(1)}, bf16[16,64]{1,0:T(8,128)(2,1)}, u32[]{:S(2)}) copy-start(bf16[16,64]{1,0:T(8,128)(2,1)} %reshape.409) | copy-start | bytes 6148
  286.7 46.9 %copy-start.142 = (bf16[16,64]{1,0:T(8,128)(2,1)S(1)}, bf16[16,64]{1,0:T(8,128)(2,1)}, u32[]{:S(2)}) copy-start(bf16[16,64]{1,0:T(8,128)(2,1)} %reshape.411) | copy-start | bytes 6148
  286.7 332.7 %all-reduce.58.cloned.1.call-start = ((), (), s32[]{:S(2)}) async-start(), calls=%async_computation.2 | async-start | bytes 786432 | tf_op jit(solution)/shard_map/psum | solution.py:226
  296.1 41.5 %copy-start.145 = (bf16[16,64]{1,0:T(8,128)(2,1)S(1)}, bf16[16,64]{1,0:T(8,128)(2,1)}, u32[]{:S(2)}) copy-start(bf16[16,64]{1,0:T(8,128)(2,1)} %reshape.413) | copy-start | bytes 6148
  409.9 10.2 %copy-start.61 = (f32[1536,3]{1,0:T(8,128)S(1)}, f32[1536,3]{1,0:T(8,128)}, u32[]{:S(2)}) copy-start(f32[1536,3]{1,0:T(8,128)} %get-tuple-element.42) | copy-start | bytes 55300
  413.6 10.2 %copy-start.136 = (f32[1536,16]{0,1:T(8,128)}, f32[1536,16]{0,1:T(8,128)S(1)}, u32[]{:S(2)}) copy-start(f32[1536,16]{0,1:T(8,128)S(1)} %fusion.29) | copy-start | bytes 294916
  414.5 19.5 %copy-start.92 = (f32[1536,16]{0,1:T(8,128)}, f32[1536,16]{0,1:T(8,128)S(1)}, u32[]{:S(2)}) copy-start(f32[1536,16]{0,1:T(8,128)S(1)} %convolution_add_fusion.27) | copy-start | bytes 294916
  419.1 13.0 %copy-start.176 = (f32[16,192]{1,0:T(8,128)S(1)}, f32[16,192]{1,0:T(8,128)}, u32[]{:S(2)}) copy-start(f32[16,192]{1,0:T(8,128)} %param.19) | copy-start | bytes 36868
  419.1 14.9 %copy-start.180 = (bf16[16,16]{1,0:T(8,128)(2,1)S(1)}, bf16[16,16]{1,0:T(8,128)(2,1)}, u32[]{:S(2)}) copy-start(bf16[16,16]{1,0:T(8,128)(2,1)} %reshape.421) | copy-start | bytes 1540
  419.1 14.9 %copy-start.217 = (f32[16]{0:T(128)S(1)}, f32[16]{0:T(128)}, u32[]{:S(2)}) copy-start(f32[16]{0:T(128)} %slice_convert_fusion) | copy-start | bytes 196
  420.1 14.5 %copy-start.158 = (bf16[4,16,16,1]{2,1,0,3:T(8,128)(2,1)S(1)}, bf16[4,16,16,1]{2,1,0,3:T(8,128)(2,1)}, u32[]{:S(2)}) copy-start(bf16[4,16,16,1]{2,1,0,3:T(8,128)(2,1)} %reshape.511) | copy-start | bytes 6148
  420.4 14.6 %copy-start.43 = (f32[8,192,4,16]{1,0,3,2:T(8,128)S(1)}, f32[8,192,4,16]{1,0,3,2:T(8,128)}, u32[]{:S(2)}) copy-start(f32[8,192,4,16]{1,0,3,2:T(8,128)} %reshape.410) | copy-start | bytes 1179652
  420.4 14.6 %copy-start.160 = (f32[8,4,192]{2,1,0:T(4,128)S(1)}, f32[8,4,192]{2,1,0:T(4,128)}, u32[]{:S(2)}) copy-start(f32[8,4,192]{2,1,0:T(4,128)} %multiply_divide_fusion.1) | copy-start | bytes 73732
  444.1 12.2 %slice-start = ((s8[6291456]{0:T(1024)(128)(4,1)}), s8[4194304]{0:T(1024)(128)(4,1)S(1)}, s32[]{:S(2)}) async-start(s8[6291456]{0:T(1024)(128)(4,1)} %bitcast.352), calls=%async_computation.3 | async-start | bytes 8388608
  456.4 10.3 %copy-start.90 = (f32[1536,16]{0,1:T(8,128)S(1)}, f32[1536,16]{0,1:T(8,128)}, u32[]{:S(2)}) copy-start(f32[1536,16]{0,1:T(8,128)} %copy-done.89) | copy-start | bytes 294916
  456.4 22.0 %slice-start.2 = ((s8[6291456]{0:T(1024)(128)(4,1)}), s8[2097152]{0:T(1024)(128)(4,1)S(1)}, s32[]{:S(2)}) async-start(s8[6291456]{0:T(1024)(128)(4,1)} %bitcast.354), calls=%async_computation.5 | async-start | bytes 4194304
  468.3 10.2 %slice-start.3 = ((s8[6291456]{0:T(1024)(128)(4,1)}), s8[4194304]{0:T(1024)(128)(4,1)S(1)}, s32[]{:S(2)}) async-start(s8[6291456]{0:T(1024)(128)(4,1)} %bitcast.354), calls=%async_computation.6 | async-start | bytes 8388608
  503.8 10.3 %copy-start.147 = (bf16[16,64]{1,0:T(8,128)(2,1)S(1)}, bf16[16,64]{1,0:T(8,128)(2,1)}, u32[]{:S(2)}) copy-start(bf16[16,64]{1,0:T(8,128)(2,1)} %reshape.413) | copy-start | bytes 6148
  504.9 10.4 %copy-start.144 = (bf16[16,64]{1,0:T(8,128)(2,1)S(1)}, bf16[16,64]{1,0:T(8,128)(2,1)}, u32[]{:S(2)}) copy-start(bf16[16,64]{1,0:T(8,128)(2,1)} %reshape.411) | copy-start | bytes 6148
  506.1 10.4 %copy-start.115 = (f32[1536,3]{0,1:T(4,128)S(1)}, f32[1536,3]{0,1:T(4,128)}, u32[]{:S(2)}) copy-start(f32[1536,3]{0,1:T(4,128)} %get-tuple-element.98) | copy-start | bytes 55300
  507.1 12.3 %copy-start.157 = (u8[1536,32]{0,1:T(8,128)(4,1)S(1)}, u8[1536,32]{0,1:T(8,128)(4,1)}, u32[]{:S(2)}) copy-start(u8[1536,32]{0,1:T(8,128)(4,1)} %copy-done.156) | copy-start | bytes 147460
  507.1 12.3 %copy-start.166 = (bf16[32,16]{1,0:T(8,128)(2,1)S(1)}, bf16[32,16]{1,0:T(8,128)(2,1)}, u32[]{:S(2)}) copy-start(bf16[32,16]{1,0:T(8,128)(2,1)} %reshape.408) | copy-start | bytes 3076
  535.1 10.9 %copy-start.98 = (f32[1536,3,16]{0,2,1:T(8,128)S(1)}, f32[1536,3,16]{0,2,1:T(8,128)}, u32[]{:S(2)}) copy-start(f32[1536,3,16]{0,2,1:T(8,128)} %copy-done.97) | copy-start | bytes 884740
  535.1 10.9 %copy-start.102 = (f32[1536,3,16]{0,2,1:T(8,128)S(1)}, f32[1536,3,16]{0,2,1:T(8,128)}, u32[]{:S(2)}) copy-start(f32[1536,3,16]{0,2,1:T(8,128)} %get-tuple-element.139) | copy-start | bytes 884740
  538.5 12.4 %copy-start.47 = (f32[1536,64]{0,1:T(8,128)}, f32[1536,64]{0,1:T(8,128)S(1)}, u32[]{:S(2)}) copy-start(f32[1536,64]{0,1:T(8,128)S(1)} %reshape.458) | copy-start | bytes 1179652
  540.8 10.1 %copy-start.21 = (f32[1536,3,32]{0,2,1:T(8,128)S(1)}, f32[1536,3,32]{0,2,1:T(8,128)}, u32[]{:S(2)}) copy-start(f32[1536,3,32]{0,2,1:T(8,128)} %copy-done.20) | copy-start | bytes 1769476
  557.1 17.3 %copy-start.159 = (f32[64,32]{1,0:T(8,128)S(1)}, f32[64,32]{1,0:T(8,128)}, u32[]{:S(2)}) copy-start(f32[64,32]{1,0:T(8,128)} %convolution_bitcast_fusion.12) | copy-start | bytes 24580
  559.1 29.7 %copy-start.94 = (f32[1536,16]{0,1:T(8,128)S(1)}, f32[1536,16]{0,1:T(8,128)}, u32[]{:S(2)}) copy-start(f32[1536,16]{0,1:T(8,128)} %copy-done.92) | copy-start | bytes 294916
  559.1 29.7 %copy-start.173 = (f32[1536]{0:T(1024)S(1)}, f32[1536]{0:T(1024)}, u32[]{:S(2)}) copy-start(f32[1536]{0:T(1024)} %copy-done.171) | copy-start | bytes 18436
  560.1 61.0 %copy-start.30 = (f32[1536,3,32]{0,2,1:T(8,128)S(1)}, f32[1536,3,32]{0,2,1:T(8,128)}, u32[]{:S(2)}) copy-start(f32[1536,3,32]{0,2,1:T(8,128)} %copy-done.29) | copy-start | bytes 1769476
  560.1 61.0 %copy-start.103 = (f32[1536,3,16]{0,2,1:T(8,128)S(1)}, f32[1536,3,16]{0,2,1:T(8,128)}, u32[]{:S(2)}) copy-start(f32[1536,3,16]{0,2,1:T(8,128)} %get-tuple-element.95) | copy-start | bytes 884740
  560.1 61.0 %copy-start.116 = (f32[1536,3]{0,1:T(4,128)S(1)}, f32[1536,3]{0,1:T(4,128)}, u32[]{:S(2)}) copy-start(f32[1536,3]{0,1:T(4,128)} %get-tuple-element.98) | copy-start | bytes 55300
  560.1 61.1 %copy-start.125 = (u8[1536,32]{0,1:T(8,128)(4,1)S(1)}, u8[1536,32]{0,1:T(8,128)(4,1)}, u32[]{:S(2)}) copy-start(u8[1536,32]{0,1:T(8,128)(4,1)} %copy-done.124) | copy-start | bytes 147460
  630.1 48.6 %copy-start.188 = (f32[1423]{0:T(1024)S(1)}, f32[1423]{0:T(1024)}, u32[]{:S(2)}) copy-start(f32[1423]{0:T(1024)} %param.12) | copy-start | bytes 17080
  630.1 48.6 %copy-start.203 = (f32[1423]{0:T(1024)S(1)}, f32[1423]{0:T(1024)}, u32[]{:S(2)}) copy-start(f32[1423]{0:T(1024)} %param.14) | copy-start | bytes 17080
  630.1 48.6 %copy-start.204 = (f32[1423]{0:T(1024)S(1)}, f32[1423]{0:T(1024)}, u32[]{:S(2)}) copy-start(f32[1423]{0:T(1024)} %param.13) | copy-start | bytes 17080
  (185 other events, 921.7 us)
Sparse Core Ops, SparseCore 0:
  207.9 32.2 all-reduce.55
  286.8 33.0 all-reduce.53
  587.3 32.0 all-reduce.57
where the time goes:
time: 699 us; the launch traced here: 687 us
  local copies, waits for them, and re-layouts  223 us (32%)
  blocking collectives  148 us (21%)
  matrix products  148 us (21%)
  other arithmetic  117 us (17%)
  waiting for transfers between devices  29.1 us (4%)
  between operations  23.1 us (3%)
    gather x6, local copies, waits for them, and re-layouts, body(): feature_maps[view_slot, :, pixel_index[start:start + point_rows]]  136 us
    dot_general x68, matrix products, matmul_low(): return jnp.matmul(left_op, right_op, precision=lax.Precision.HIGHEST)  71.2 us
    dot_general x8, matrix products, ray_part(): jnp.einsum('rhqk,rkhd->rqhd', attention, val_rows, precision=lax.Precisio...  39.1 us
    unnamed x1, blocking collectives  38.8 us
    psum x1, blocking collectives, body(): loss = lax.psum(loss_part, 'rays') * seed  37.6 us
    dot_general x8, matrix products, ray_part(): jnp.einsum('rqhd,rkhd->rhqk', queries, key_rows, precision=lax.Precision....  37.4 us
    psum x1, blocking collectives, body(): lax.psum((numerator, denominator, colour_sum), 'views')  36.2 us
    reduce_sum x4, other arithmetic, blend_part(): colour_sum = jnp.sum(exponent[..., :1] * colour_in, axis=1)  29.2 us
  transfers between devices with their start and end apart: 3, of which 1 were waited for; matrix products, arithmetic and copies ran while one was open for 4% of the time, Pallas kernels for 0%

commit v1 on v0

--- a/solution.py
+++ b/solution.py
@@ -223,7 +223,9 @@
         )
         own_gsum, own_gsquare = back_moments((grad_average, grad_variance))
         grad_sum, grad_square = (
-            lax.psum(own_gsum.astype(jnp.bfloat16), "views").astype(jnp.float32),
+            jnp.sum(lax.all_gather(own_gsum.astype(jnp.bfloat16), "views"), axis=0).astype(
+                jnp.float32
+            ),
             lax.psum(own_gsquare.astype(jnp.bfloat16), "views").astype(jnp.float32),
         )
         (grad_view_w,) = back_views((grad_feature, grad_sum, grad_square))

time: 699 us -> 715 us (1.023)
  blocking collectives: 148 us -> 161 us
    all_gather x0 -> x2, blocking collectives: none -> 13.6 us  [body(): lax.all_gather(own_gsum.astype(jnp.bfloat16), 'views')]
    unnamed x467 -> x487, local copies, waits for them, and re-layouts: 19 us -> 19.1 us
where the time goes in v1:
time: 715 us; the launch traced here: 703 us
  local copies, waits for them, and re-layouts  223 us (31%)
  blocking collectives  161 us (23%)
  matrix products  147 us (21%)
  other arithmetic  120 us (17%)
  waiting for transfers between devices  27.6 us (4%)
  between operations  23.3 us (3%)
    gather x6, local copies, waits for them, and re-layouts, body(): feature_maps[view_slot, :, pixel_index[start:start + point_rows]]  135 us
    dot_general x68, matrix products, matmul_low(): return jnp.matmul(left_op, right_op, precision=lax.Precision.HIGHEST)  71 us
    dot_general x8, matrix products, ray_part(): jnp.einsum('rhqk,rkhd->rqhd', attention, val_rows, precision=lax.Precisio...  39 us
    unnamed x1, blocking collectives  38.8 us
    psum x1, blocking collectives, body(): loss = lax.psum(loss_part, 'rays') * seed  37.6 us
    dot_general x8, matrix products, ray_part(): jnp.einsum('rqhd,rkhd->rhqk', queries, key_rows, precision=lax.Precision....  37.4 us
    psum x1, blocking collectives, body(): lax.psum((numerator, denominator, colour_sum), 'views')  36.2 us
    reduce_sum x4, other arithmetic, blend_part(): colour_sum = jnp.sum(exponent[..., :1] * colour_in, axis=1)  29.1 us
  transfers between devices with their start and end apart: 3, of which 1 were waited for; matrix products, arithmetic and copies ran while one was open for 4% of the time, Pallas kernels for 0%

profile of v1, /device:TPU:0, one launch (start us, length us, event | category | flops | bytes accessed | tf_op | source)
XLA Modules:
  0.0 702.8 jit_solution(5593170361859144277)
XLA Ops:
  10.2 38.8 %all-reduce.42 = bf16[11384]{0:T(1024)(128)(2,1)S(1)} all-reduce(bf16[11384]{0:T(1024)(128)(2,1)S(1)} %dynamic-update-slice), channel_id=1, replica_groups=mesh['rays'=8,'views'=4] {'rays'}, use_global_device_ids=true, to_apply=%add.42 | all-reduce | flops 11384 | bytes 45536
  50.5 8.6 %copy.206 = bf16[3,35,12032]{1,2,0:T(8,128)(2,1)} copy(bf16[3,35,12032]{2,1,0:T(8,128)(2,1)} %param.16) | data formatting | bytes 5053440 | tf_op args[4]
  59.8 54.3 %gather_fusion = bf16[4608,35]{1,0:T(8,128)(2,1)S(1)} fusion(bf16[3,35,12032]{1,2,0:T(8,128)(2,1)} %copy.206, s32[4608]{0:T(1024)S(1)} %reshape.470), kind=kCustom, calls=%fused_computation | custom fusion | bytes 681984 | tf_op jit(solution)/shard_map/gather | solution.py:165
  121.4 75.2 %gather_fusion.1 = bf16[4608,35]{1,0:T(8,128)(2,1)} fusion(bf16[3,35,12032]{1,2,0:T(8,128)(2,1)} %copy.206, s32[4608]{0:T(1024)S(1)} %reshape.476), kind=kCustom, calls=%fused_computation.1 | custom fusion | bytes 681984 | tf_op jit(solution)/shard_map/gather | solution.py:165
  196.6 3.3 reshape.479
  220.2 17.7 %psum.132 = f32[]{:T(128)} all-reduce(f32[]{:T(128)} %get-tuple-element.34), channel_id=1, replica_groups=mesh['rays'=8,'views'=4] {'rays'}, use_global_device_ids=true, to_apply=%region_45.47 | all-reduce | flops 1 | bytes 8 | tf_op jit(solution)/shard_map/psum | solution.py:157
  240.8 11.5 %all-reduce.46 = (f32[1536]{0:T(1024)}, f32[1536]{0:T(1024)}) all-reduce(f32[1536]{0:T(1024)} %get-tuple-element.28, f32[1536]{0:T(1024)} %get-tuple-element.29), channel_id=1, replica_groups=mesh['rays'=8,'views'=4] {'views'}, use_global_device_ids=true, to_apply=%region_25.27 | all-reduce | flops 3072 | bytes 24576 | tf_op jit(solution)/shard_map/psum | solution.py:179
  262.6 2.2 fusion.134
  271.8 10.6 %fusion.16 = f32[1536,3]{1,0:T(8,128)} fusion(f32[1536,3]{1,0:T(8,128)} %bitcast.367, bf16[1536,3,35]{2,1,0:T(4,128)(2,1)S(1)} %reshape.473), kind=kLoop, calls=%fused_computation.28 | loop fusion | flops 36864 | bytes 64512 | tf_op jit(solution)/shard_map/jvp()/reduce_sum | solution.py:82
  286.8 9.3 %fusion.18 = f32[1536,3]{1,0:T(8,128)} fusion(f32[1536,3]{1,0:T(8,128)S(1)} %bitcast.364, bf16[1536,3,35]{2,1,0:T(4,128)(2,1)S(1)} %reshape.479), kind=kLoop, calls=%fused_computation.30 | loop fusion | flops 36864 | bytes 64512 | tf_op jit(solution)/shard_map/jvp()/reduce_sum | solution.py:82
  296.1 36.2 %all-reduce.45 = (f32[1536,3]{1,0:T(8,128)}, f32[1536,3]{1,0:T(8,128)}) all-reduce(f32[1536,3]{1,0:T(8,128)} %fusion.18, f32[1536,3]{1,0:T(8,128)S(1)} %copy-done.63), channel_id=1, replica_groups=mesh['rays'=8,'views'=4] {'views'}, use_global_device_ids=true, to_apply=%region_39.41 | all-reduce | flops 9216 | bytes 73728 | tf_op jit(solution)/shard_map/psum | solution.py:202
  344.9 5.3 fusion.96
  350.2 5.3 fusion.258
  356.5 5.3 fusion.255
  364.7 3.3 convolution_bitcast_fusion.9
  381.4 5.5 fusion.104
  386.9 5.3 fusion.251
  393.3 5.3 fusion.248
  401.8 3.3 convolution_bitcast_fusion.11
  421.7 2.3 multiply_reduce_fusion.8
  424.1 2.9 reduce-window.36
  427.2 2.3 multiply_reduce_fusion.9
  429.7 2.5 reduce-window.34
  435.4 8.9 %multiply_reduce_fusion.1 = (f32[8,4,192]{2,1,0:T(4,128)S(1)}, f32[8,4,192,192]{2,3,1,0:T(8,128)S(1)}) fusion(f32[8,4,192,192]{2,3,1,0:T(8,128)} %copy-done.3, f32[8,4,192]{2,1,0:T(4,128)S(1)} %copy-done.163, f32[8,4,16,192]{3,2,1,0:T(8,128)S(1)} %convolution_bitcast_fusion.7, f32[8,192,4,16]{1,0,3,2:T(8,128)S(1)} %copy-done.43), kind=kOutput, calls=%fused_computation.9 | convolution fusion | flops 230025216 | bytes 10272768 | tf_op jit(solution)/shard_map/transpose(jvp(rhqk,rkhd->rqhd))/dot_general | solution.py:104
  444.4 5.0 convolution_bitcast_fusion.4
  449.5 7.2 %convolution_bitcast_fusion.5 = f32[8,192,4,16]{1,3,2,0:T(8,128)} fusion(f32[8,192,4,16]{1,0,3,2:T(8,128)S(1)} %copy-done.78, f32[8,4,192,192]{2,3,1,0:T(8,128)S(1)} %bitcast.361, f32[8,4,192,192]{2,3,1,0:T(8,128)S(1)} %get-tuple-element.177, f32[8,4,192]{2,1,0:T(4,128)S(1)} %neg.100, f32[8,4,192]{2,1,0:T(4,128)S(1)} %copy-done.145), kind=kOutput, calls=%fused_computation.83 | convolution fusion | flops 231211008 | bytes 10272768 | tf_op jit(solution)/shard_map/transpose(jvp(rqhd,rkhd->rhqk))/dot_general | solution.py:101
  456.7 6.4 convolution_bitcast_fusion.6
  464.4 2.1 fusion.236
  470.0 8.9 %convolution_bitcast_fusion.2 = f32[8,192,4,16]{1,3,2,0:T(8,128)} fusion(f32[8,4,16,192]{3,2,1,0:T(8,128)S(1)} %convolution_bitcast_fusion.3, f32[8,4,192,192]{2,3,1,0:T(8,128)} %copy-done), kind=kOutput, calls=%fused_computation.80 | convolution fusion | flops 226492416 | bytes 5505024 | tf_op jit(solution)/shard_map/transpose(jvp(rhqk,rkhd->rqhd))/dot_general | solution.py:104
  478.9 6.2 multiply_reduce_fusion
  485.2 7.3 %convolution_bitcast_fusion.1 = f32[8,192,4,16]{1,3,2,0:T(8,128)} fusion(f32[8,192,4,16]{1,0,3,2:T(8,128)S(1)} %copy-done.74, f32[8,4,192,192]{2,3,1,0:T(8,128)S(1)} %bitcast.359, f32[8,4,192,192]{2,3,1,0:T(8,128)S(1)} %get-tuple-element.172, f32[8,4,192]{2,1,0:T(4,128)S(1)} %neg.109, f32[8,4,192]{2,1,0:T(4,128)S(1)} %copy-done.143), kind=kOutput, calls=%fused_computation.79 | convolution fusion | flops 231211008 | bytes 10272768 | tf_op jit(solution)/shard_map/transpose(jvp(rqhd,rkhd->rhqk))/dot_general | solution.py:101
  492.4 5.1 convolution_bitcast_fusion
  500.1 2.1 copy.249
  502.2 2.0 reshape.442
  507.5 5.4 fusion.17
  517.0 2.7 fusion.230
  530.3 3.8 fusion.19
  538.8 2.3 copy.271
  541.1 2.0 reshape.459
  546.4 2.5 fusion.235
  549.0 2.3 fusion.260
  562.2 6.4 all-gather
  584.0 7.3 %all-gather.1 = bf16[6144,32]{0,1:T(8,128)(2,1)} all-gather(bf16[1536,32]{0,1:T(8,128)(2,1)S(1)} %get-tuple-element.84), channel_id=3, replica_groups=mesh['rays'=8,'views'=4] {'views'}, dimensions={0}, use_global_device_ids=true | all-gather | bytes 491520 | tf_op jit(solution)/shard_map/all_gather | solution.py:226
  606.1 27.5 %all-reduce.58.cloned.1.call-done = (bf16[1536,32]{0,1:T(8,128)(2,1)}, bf16[1536,32]{0,1:T(8,128)(2,1)}) async-done(((bf16[1536,32]{0,1:T(8,128)(2,1)}, bf16[1536,32]{0,1:T(8,128)(2,1)}), (bf16[1536,32]{0,1:T(8,128)(2,1)}, bf16[1536,32]{0,1:T(8,128)(2,1)})) %all-reduce.58.cloned.1.call-update) | async-done | bytes 196624 | tf_op jit(solution)/shard_map/psum | solution.py:229
  634.6 2.3 fusion.228
  636.9 3.7 convolution_bitcast_fusion.15
  649.8 37.6 %all-reduce.44 = (f32[]{:T(128)}, f32[11384]{0:T(1024)S(1)}) all-reduce(f32[]{:T(128)S(6)} %add.404, f32[11384]{0:T(1024)S(1)} %multiply_add_fusion), channel_id=1, replica_groups=mesh['rays'=8,'views'=4] {'rays'}, use_global_device_ids=true, to_apply=%region_43.45 | all-reduce | flops 11385 | bytes 91080 | tf_op jit(solution)/shard_map/psum | solution.py:235
  687.4 6.0 psum.135
  (754 shorter events, 190.3 us)
Async XLA Ops:
  7.2 248.4 %all-reduce.56.cloned.1.call-start = ((), (), s32[]{:S(2)}) async-start(), calls=%async_computation.1 | async-start | bytes 1572864 | tf_op jit(solution)/shard_map/psum | solution.py:179
  114.9 156.9 %copy-start.6 = (bf16[1536,3,35]{2,1,0:T(4,128)(2,1)}, bf16[1536,3,35]{2,1,0:T(4,128)(2,1)S(1)}, u32[]{:S(2)}) copy-start(bf16[1536,3,35]{2,1,0:T(4,128)(2,1)S(1)} %reshape.473) | copy-start | bytes 967684
  120.6 85.9 %copy-start.113 = (f32[1536,3]{0,1:T(4,128)}, f32[1536,3]{0,1:T(4,128)S(1)}, u32[]{:S(2)}) copy-start(f32[1536,3]{0,1:T(4,128)S(1)} %get-tuple-element.95) | copy-start | bytes 55300
  199.9 86.8 %copy-start.4 = (bf16[1536,3,35]{2,1,0:T(4,128)(2,1)}, bf16[1536,3,35]{2,1,0:T(4,128)(2,1)S(1)}, u32[]{:S(2)}) copy-start(bf16[1536,3,35]{2,1,0:T(4,128)(2,1)S(1)} %reshape.479) | copy-start | bytes 967684
  207.7 124.6 %all-reduce.54.cloned.1.call-start = ((), (), s32[]{:S(2)}) async-start(), calls=%async_computation | async-start | bytes 786432 | tf_op jit(solution)/shard_map/psum | solution.py:202
  220.2 35.3 %copy-start.204 = (f32[16]{0:T(128)}, f32[16]{0:T(128)S(1)}, u32[]{:S(2)}) copy-start(f32[16]{0:T(128)S(1)} %get-tuple-element.35) | copy-start | bytes 196
  268.5 15.2 %copy-start.114 = (f32[1536,3]{0,1:T(4,128)S(1)}, f32[1536,3]{0,1:T(4,128)}, u32[]{:S(2)}) copy-start(f32[1536,3]{0,1:T(4,128)} %copy-done.113) | copy-start | bytes 55300
  271.8 10.6 %copy-start.25 = (f32[1536,3,32]{0,2,1:T(8,128)S(1)}, f32[1536,3,32]{0,2,1:T(8,128)}, u32[]{:S(2)}) copy-start(f32[1536,3,32]{0,2,1:T(8,128)} %copy-done.24) | copy-start | bytes 1769476
  271.8 10.6 %copy-start.70 = (f32[1536,3,32]{0,2,1:T(8,128)S(1)}, f32[1536,3,32]{0,2,1:T(8,128)}, u32[]{:S(2)}) copy-start(f32[1536,3,32]{0,2,1:T(8,128)} %get-tuple-element.136) | copy-start | bytes 1769476
  271.8 10.6 %copy-start.158 = (u8[1536,32]{0,1:T(8,128)(4,1)S(1)}, u8[1536,32]{0,1:T(8,128)(4,1)}, u32[]{:S(2)}) copy-start(u8[1536,32]{0,1:T(8,128)(4,1)} %get-tuple-element.135) | copy-start | bytes 147460
  271.8 12.0 %copy-start.68 = (f32[1536,3,32]{0,2,1:T(8,128)S(1)}, f32[1536,3,32]{0,2,1:T(8,128)}, u32[]{:S(2)}) copy-start(f32[1536,3,32]{0,2,1:T(8,128)} %get-tuple-element.80) | copy-start | bytes 1769476
  283.0 13.1 %copy-start.63 = (f32[1536,3]{1,0:T(8,128)S(1)}, f32[1536,3]{1,0:T(8,128)}, u32[]{:S(2)}) copy-start(f32[1536,3]{1,0:T(8,128)} %fusion.16) | copy-start | bytes 55300
  286.3 46.9 %copy-start.152 = (bf16[16,64]{1,0:T(8,128)(2,1)S(1)}, bf16[16,64]{1,0:T(8,128)(2,1)}, u32[]{:S(2)}) copy-start(bf16[16,64]{1,0:T(8,128)(2,1)} %reshape.409) | copy-start | bytes 6148
  286.7 46.9 %copy-start.146 = (bf16[16,64]{1,0:T(8,128)(2,1)S(1)}, bf16[16,64]{1,0:T(8,128)(2,1)}, u32[]{:S(2)}) copy-start(bf16[16,64]{1,0:T(8,128)(2,1)} %reshape.411) | copy-start | bytes 6148
  286.7 346.9 %all-reduce.58.cloned.1.call-start = ((), (), s32[]{:S(2)}) async-start(), calls=%async_computation.2 | async-start | bytes 393216 | tf_op jit(solution)/shard_map/psum | solution.py:229
  296.1 41.5 %copy-start.149 = (bf16[16,64]{1,0:T(8,128)(2,1)S(1)}, bf16[16,64]{1,0:T(8,128)(2,1)}, u32[]{:S(2)}) copy-start(bf16[16,64]{1,0:T(8,128)(2,1)} %reshape.413) | copy-start | bytes 6148
  414.6 19.8 %copy-start.93 = (f32[1536,16]{0,1:T(8,128)}, f32[1536,16]{0,1:T(8,128)S(1)}, u32[]{:S(2)}) copy-start(f32[1536,16]{0,1:T(8,128)S(1)} %convolution_add_fusion.27) | copy-start | bytes 294916
  419.3 13.0 %copy-start.180 = (f32[16,192]{1,0:T(8,128)S(1)}, f32[16,192]{1,0:T(8,128)}, u32[]{:S(2)}) copy-start(f32[16,192]{1,0:T(8,128)} %param.19) | copy-start | bytes 36868
  419.3 15.0 %copy-start.184 = (bf16[16,16]{1,0:T(8,128)(2,1)S(1)}, bf16[16,16]{1,0:T(8,128)(2,1)}, u32[]{:S(2)}) copy-start(bf16[16,16]{1,0:T(8,128)(2,1)} %reshape.421) | copy-start | bytes 1540
  419.4 15.0 %copy-start.227 = (f32[16]{0:T(128)S(1)}, f32[16]{0:T(128)}, u32[]{:S(2)}) copy-start(f32[16]{0:T(128)} %slice_convert_fusion) | copy-start | bytes 196
  420.3 14.6 %copy-start.162 = (bf16[4,16,16,1]{2,1,0,3:T(8,128)(2,1)S(1)}, bf16[4,16,16,1]{2,1,0,3:T(8,128)(2,1)}, u32[]{:S(2)}) copy-start(bf16[4,16,16,1]{2,1,0,3:T(8,128)(2,1)} %reshape.513) | copy-start | bytes 6148
  420.6 14.7 %copy-start.43 = (f32[8,192,4,16]{1,0,3,2:T(8,128)S(1)}, f32[8,192,4,16]{1,0,3,2:T(8,128)}, u32[]{:S(2)}) copy-start(f32[8,192,4,16]{1,0,3,2:T(8,128)} %reshape.410) | copy-start | bytes 1179652
  420.6 14.7 %copy-start.163 = (f32[8,4,192]{2,1,0:T(4,128)S(1)}, f32[8,4,192]{2,1,0:T(4,128)}, u32[]{:S(2)}) copy-start(f32[8,4,192]{2,1,0:T(4,128)} %multiply_divide_fusion.1) | copy-start | bytes 73732
  444.4 12.2 %slice-start = ((s8[6291456]{0:T(1024)(128)(4,1)}), s8[4194304]{0:T(1024)(128)(4,1)S(1)}, s32[]{:S(2)}) async-start(s8[6291456]{0:T(1024)(128)(4,1)} %bitcast.356), calls=%async_computation.3 | async-start | bytes 8388608
  456.6 10.5 %copy-start.90 = (f32[1536,16]{0,1:T(8,128)S(1)}, f32[1536,16]{0,1:T(8,128)}, u32[]{:S(2)}) copy-start(f32[1536,16]{0,1:T(8,128)} %copy-done.89) | copy-start | bytes 294916
  456.7 22.2 %slice-start.2 = ((s8[6291456]{0:T(1024)(128)(4,1)}), s8[2097152]{0:T(1024)(128)(4,1)S(1)}, s32[]{:S(2)}) async-start(s8[6291456]{0:T(1024)(128)(4,1)} %bitcast.358), calls=%async_computation.5 | async-start | bytes 4194304
  505.3 10.4 %copy-start.148 = (bf16[16,64]{1,0:T(8,128)(2,1)S(1)}, bf16[16,64]{1,0:T(8,128)(2,1)}, u32[]{:S(2)}) copy-start(bf16[16,64]{1,0:T(8,128)(2,1)} %reshape.411) | copy-start | bytes 6148
  506.6 10.4 %copy-start.118 = (f32[1536,3]{0,1:T(4,128)S(1)}, f32[1536,3]{0,1:T(4,128)}, u32[]{:S(2)}) copy-start(f32[1536,3]{0,1:T(4,128)} %get-tuple-element.96) | copy-start | bytes 55300
  507.5 12.2 %copy-start.161 = (u8[1536,32]{0,1:T(8,128)(4,1)S(1)}, u8[1536,32]{0,1:T(8,128)(4,1)}, u32[]{:S(2)}) copy-start(u8[1536,32]{0,1:T(8,128)(4,1)} %copy-done.160) | copy-start | bytes 147460
  507.5 12.2 %copy-start.168 = (bf16[32,16]{1,0:T(8,128)(2,1)S(1)}, bf16[32,16]{1,0:T(8,128)(2,1)}, u32[]{:S(2)}) copy-start(bf16[32,16]{1,0:T(8,128)(2,1)} %reshape.408) | copy-start | bytes 3076
  535.4 10.9 %copy-start.100 = (f32[1536,3,16]{0,2,1:T(8,128)S(1)}, f32[1536,3,16]{0,2,1:T(8,128)}, u32[]{:S(2)}) copy-start(f32[1536,3,16]{0,2,1:T(8,128)} %copy-done.99) | copy-start | bytes 884740
  535.4 10.9 %copy-start.104 = (f32[1536,3,16]{0,2,1:T(8,128)S(1)}, f32[1536,3,16]{0,2,1:T(8,128)}, u32[]{:S(2)}) copy-start(f32[1536,3,16]{0,2,1:T(8,128)} %get-tuple-element.137) | copy-start | bytes 884740
  538.8 12.5 %copy-start.46 = (f32[1536,64]{0,1:T(8,128)}, f32[1536,64]{0,1:T(8,128)S(1)}, u32[]{:S(2)}) copy-start(f32[1536,64]{0,1:T(8,128)S(1)} %reshape.458) | copy-start | bytes 1179652
  560.4 11.3 %copy-start.178 = (f32[32,16]{1,0:T(8,128)S(1)}, f32[32,16]{1,0:T(8,128)}, u32[]{:S(2)}) copy-start(f32[32,16]{1,0:T(8,128)} %convolution_bitcast_fusion.19) | copy-start | bytes 6148
  561.5 12.4 %copy-start.96 = (f32[1536,16]{0,1:T(8,128)S(1)}, f32[1536,16]{0,1:T(8,128)}, u32[]{:S(2)}) copy-start(f32[1536,16]{0,1:T(8,128)} %copy-done.93) | copy-start | bytes 294916
  568.9 35.6 %copy-start.92 = (f32[1536,16]{0,1:T(8,128)S(1)}, f32[1536,16]{0,1:T(8,128)}, u32[]{:S(2)}) copy-start(f32[1536,16]{0,1:T(8,128)} %copy-done.89) | copy-start | bytes 294916
  568.9 65.6 %copy-start.30 = (f32[1536,3,32]{0,2,1:T(8,128)S(1)}, f32[1536,3,32]{0,2,1:T(8,128)}, u32[]{:S(2)}) copy-start(f32[1536,3,32]{0,2,1:T(8,128)} %copy-done.29) | copy-start | bytes 1769476
  572.4 22.9 %copy-start.179 = (f32[32,16]{1,0:T(8,128)S(1)}, f32[32,16]{1,0:T(8,128)}, u32[]{:S(2)}) copy-start(f32[32,16]{1,0:T(8,128)} %convolution_bitcast_fusion.18) | copy-start | bytes 6148
  575.5 27.0 %copy-start.205 = (f32[16]{0:T(128)S(1)}, f32[16]{0:T(128)}, u32[]{:S(2)}) copy-start(f32[16]{0:T(128)} %copy-done.204) | copy-start | bytes 196
  575.5 27.0 %copy-start.223 = (f32[8]{0:T(128)S(1)}, f32[8]{0:T(128)}, u32[]{:S(2)}) copy-start(f32[8]{0:T(128)} %get-tuple-element.118) | copy-start | bytes 100
  575.5 27.0 %copy-start.224 = (f32[8]{0:T(128)S(1)}, f32[8]{0:T(128)}, u32[]{:S(2)}) copy-start(f32[8]{0:T(128)} %get-tuple-element.185) | copy-start | bytes 100
  575.5 29.0 %copy-start.193 = (f32[1536,1]{0,1:T(1,128)S(1)}, f32[1536,1]{0,1:T(1,128)}, u32[]{:S(2)}) copy-start(f32[1536,1]{0,1:T(1,128)} %reshape.531) | copy-start | bytes 18436
  575.5 59.1 %copy-start.119 = (f32[1536,3]{0,1:T(4,128)S(1)}, f32[1536,3]{0,1:T(4,128)}, u32[]{:S(2)}) copy-start(f32[1536,3]{0,1:T(4,128)} %get-tuple-element.96) | copy-start | bytes 55300
  575.5 59.1 %copy-start.128 = (u8[1536,32]{0,1:T(8,128)(4,1)S(1)}, u8[1536,32]{0,1:T(8,128)(4,1)}, u32[]{:S(2)}) copy-start(u8[1536,32]{0,1:T(8,128)(4,1)} %copy-done.127) | copy-start | bytes 147460
  593.7 43.2 %copy-start.132 = (u8[1536,64]{0,1:T(8,128)(4,1)S(1)}, u8[1536,64]{0,1:T(8,128)(4,1)}, u32[]{:S(2)}) copy-start(u8[1536,64]{0,1:T(8,128)(4,1)} %copy-done.130) | copy-start | bytes 294916
  645.4 48.7 %copy-start.192 = (f32[1423]{0:T(1024)S(1)}, f32[1423]{0:T(1024)}, u32[]{:S(2)}) copy-start(f32[1423]{0:T(1024)} %param.12) | copy-start | bytes 17080
  645.4 48.7 %copy-start.209 = (f32[1423]{0:T(1024)S(1)}, f32[1423]{0:T(1024)}, u32[]{:S(2)}) copy-start(f32[1423]{0:T(1024)} %param.14) | copy-start | bytes 17080
  645.4 48.7 %copy-start.210 = (f32[1423]{0:T(1024)S(1)}, f32[1423]{0:T(1024)}, u32[]{:S(2)}) copy-start(f32[1423]{0:T(1024)} %param.13) | copy-start | bytes 17080
  (195 other events, 1018.0 us)
Sparse Core Ops, SparseCore 0:
  207.8 32.3 all-reduce.55
  286.8 33.0 all-reduce.53
  602.6 31.0 all-reduce.57
